TPU v7x, 256 devices: a whole 4x4x8 slice. The times are simulated.
256 devices in a mesh: section: 8 (over z), tm: 32 (over x, y, core).
Axes of the slice: x: 4, y: 4, z: 8, core: 2. Of those that a mesh axis runs over, the one named last changes fastest.
Arguments:
- acts: bfloat16 [8, 2, 2048, 1024], P('section', None, 'tm'), may hold values from -600 to 600
- grad_top: bfloat16 [2, 2048, 1024], P(None, 'tm'), may hold values from -6 to 6
- w_in: bfloat16 [8, 1024, 3072], P('section'), may hold values from -0.1875 to 0.1875
- w_out: bfloat16 [8, 1024, 1024], P('section'), may hold values from -0.1875 to 0.1875
- offsets: int32 [32, 5], P('tm'), may hold values from 0 to 16, as said below
Outputs:
- d_acts: bfloat16 [8, 2, 2048, 1024], P('section', None, 'tm')
- d_w_in: float32 [8, 1024, 3072], P('section', 'tm')
- d_w_out: float32 [8, 1024, 1024], P('section', 'tm')
Inputs may be any that keep to these rules, and one draw needn't show every extreme that they name: offsets[t, k] is 0 or 2**k, and 0 wherever t < 2**k; the last shard uses every level.
All inputs are finite; a program needn't handle non-finite values.
Results may differ from a plain program's by a relative error of at most 0.018.
The roundings to bfloat16 on the way count: a program that leaves them out, or rounds other values in their place, can miss the bound.
Values may be sent and summed in bfloat16 or wider, within the bound.
A program may use at most 128 MiB of HBM per device.

v0:
```python
import jax
import jax.numpy as jnp
from jax import lax
from jax.sharding import PartitionSpec as P

HEAD_DIM = 64
epsilon = 1e-06
negative_fill = -1e30


def shifted(value, axis, steps):
    count = lax.axis_size(axis)
    initial, last = (max(0, -steps), min(count, count - steps))
    return lax.ppermute(value, axis, [(source, source + steps) for source in range(initial, last)])


def normalize(inputs):
    values = inputs.astype(jnp.float32)
    inverse_rms = lax.rsqrt(jnp.mean(values * values, axis=-1, keepdims=True) + epsilon)
    return (values * inverse_rms, inverse_rms)


def key_bias(level_flags, shard_rows):
    position = jnp.arange(shard_rows)
    own_part = position[None, :] <= position[:, None]
    far_part = jnp.repeat(level_flags != 0, shard_rows)
    far_part = jnp.broadcast_to(far_part[None, :], (shard_rows, far_part.shape[0]))
    return jnp.concatenate([own_part, far_part], 1)


def split_heads(row_block):
    return row_block.reshape(row_block.shape[0], -1, HEAD_DIM)


def softmax_keys(queries, key_heads, allowed):
    scores = jnp.einsum(
        "ihd,jhd->hij", queries, key_heads, preferred_element_type=jnp.float32
    ) * HEAD_DIM ** (-0.5)
    scores = jnp.where(allowed[None], scores, negative_fill)
    highest = jnp.max(scores, axis=-1, keepdims=True)
    shifted_exp = jnp.where(allowed[None], jnp.exp(scores - highest), 0.0)
    return shifted_exp / jnp.sum(shifted_exp, axis=-1, keepdims=True)


def attend(query_rows, key_rows, allowed):
    model_width = query_rows.shape[1]
    probability = softmax_keys(
        split_heads(query_rows), split_heads(key_rows[:, :model_width]), allowed
    )
    attended = jnp.einsum(
        "hij,jhd->ihd",
        probability.astype(jnp.bfloat16),
        split_heads(key_rows[:, model_width:]),
        preferred_element_type=jnp.float32,
    )
    return attended.reshape(query_rows.shape).astype(jnp.bfloat16)


def attend_back(query_rows, key_rows, allowed, incoming, attended, w_proj):
    model_width = query_rows.shape[1]
    queries = split_heads(query_rows)
    key_heads = split_heads(key_rows[:, :model_width])
    value_heads = split_heads(key_rows[:, model_width:])
    probability = softmax_keys(queries, key_heads, allowed)
    rounded = probability.astype(jnp.bfloat16)
    upstream = lax.dot_general(
        incoming, w_proj, (((1,), (1,)), ((), ())), preferred_element_type=jnp.float32
    ).astype(jnp.bfloat16)
    up_heads = split_heads(upstream)
    delta = jnp.einsum(
        "ihd,ihd->hi", up_heads.astype(jnp.float32), split_heads(attended).astype(jnp.float32)
    )[..., None]
    prob_grad = jnp.einsum(
        "ihd,jhd->hij", up_heads, value_heads, preferred_element_type=jnp.float32
    )
    score_grad = (probability * (prob_grad - delta)).astype(jnp.bfloat16)
    scale_factor = HEAD_DIM ** (-0.5)
    query_grad = (
        jnp.einsum("hij,jhd->ihd", score_grad, key_heads, preferred_element_type=jnp.float32)
        * scale_factor
    )
    key_grad = (
        jnp.einsum("hij,ihd->jhd", score_grad, queries, preferred_element_type=jnp.float32)
        * scale_factor
    )
    value_grad = jnp.einsum("hij,ihd->jhd", rounded, up_heads, preferred_element_type=jnp.float32)
    return (
        query_grad.reshape(-1, model_width),
        key_grad.reshape(-1, model_width),
        value_grad.reshape(-1, model_width),
    )


def per_device(acts, grad_top, w_in, w_out, offsets):
    sections = lax.axis_size("section")
    shards = lax.axis_size("tm")
    levels = shards.bit_length() - 1
    section_index = lax.axis_index("section")
    micro_count = acts.shape[1]
    shard_rows = acts.shape[2]
    model_width = acts.shape[3]
    w_qkv = w_in[0]
    w_proj = w_out[0]
    level_flags = offsets[0]
    normed, inverse_rms = normalize(acts[0])
    rounded_norm = normed.astype(jnp.bfloat16)
    qkv = jnp.dot(rounded_norm.reshape(-1, model_width), w_qkv, preferred_element_type=jnp.float32)
    qkv = qkv.astype(jnp.bfloat16).reshape(micro_count, shard_rows, 3 * model_width)
    pairs = qkv[..., model_width:]
    every_pair = lax.all_gather(pairs, "tm", axis=1, tiled=True)
    shard_index = lax.axis_index("tm")
    far_list = []
    for level in range(levels):
        source = jnp.maximum(shard_index - 2**level, 0) * shard_rows
        far_list.append(lax.dynamic_slice_in_dim(every_pair, source, shard_rows, 1))
    key_rows = jnp.concatenate([pairs] + far_list, 1)
    allowed = key_bias(level_flags, shard_rows)
    attended = jnp.stack(
        [
            attend(qkv[index, :, :model_width], key_rows[index], allowed)
            for index in range(micro_count)
        ],
        0,
    )

    def attention_part(incoming, slot):
        query_rows = lax.dynamic_index_in_dim(qkv, slot, 0, False)[:, :model_width]
        slot_keys = lax.dynamic_index_in_dim(key_rows, slot, 0, False)
        slot_attended = lax.dynamic_index_in_dim(attended, slot, 0, False)
        query_grad, key_grad, value_grad = attend_back(
            query_rows, slot_keys, allowed, incoming, slot_attended, w_proj
        )
        owner_sum = jnp.concatenate([key_grad[:shard_rows], value_grad[:shard_rows]], 1)
        far_part = jnp.concatenate([key_grad[shard_rows:], value_grad[shard_rows:]], 1)
        far_part = far_part.astype(jnp.bfloat16).reshape(levels, shard_rows, 2 * model_width)
        return (query_grad, owner_sum, far_part)

    def empty_attention(incoming, slot):
        return (
            jnp.zeros((shard_rows, model_width), jnp.float32),
            jnp.zeros((shard_rows, 2 * model_width), jnp.float32),
            jnp.zeros((levels, shard_rows, 2 * model_width), jnp.bfloat16),
        )

    def norm_part(qkv_grad, incoming, slot):
        norm_grad = lax.dot_general(
            qkv_grad, w_qkv, (((1,), (1,)), ((), ())), preferred_element_type=jnp.float32
        )
        slot_normed = lax.dynamic_index_in_dim(normed, slot, 0, False)
        slot_rms = lax.dynamic_index_in_dim(inverse_rms, slot, 0, False)
        inner = jnp.mean(norm_grad * slot_normed, axis=-1, keepdims=True)
        return (incoming.astype(jnp.float32) + slot_rms * (norm_grad - slot_normed * inner)).astype(
            jnp.bfloat16
        )

    def empty_norm(qkv_grad, incoming, slot):
        return jnp.zeros((shard_rows, model_width), jnp.bfloat16)

    def step(turn, carry):
        received, grad_store, qkv_store, incoming_store = carry
        slot_raw = turn - (sections - 1 - section_index)
        active = (slot_raw >= 0) & (slot_raw < micro_count)
        slot = jnp.clip(slot_raw, 0, micro_count - 1)
        incoming = jnp.where(
            section_index == sections - 1,
            lax.dynamic_index_in_dim(grad_top, slot, 0, False),
            received,
        )
        query_grad, owner_sum, far_part = lax.cond(
            active, attention_part, empty_attention, incoming, slot
        )
        for level in range(levels):
            owner_sum = owner_sum + shifted(far_part[level], "tm", -(2**level)).astype(jnp.float32)
        qkv_grad = jnp.concatenate([query_grad, owner_sum], 1).astype(jnp.bfloat16)
        grad_in = lax.cond(active, norm_part, empty_norm, qkv_grad, incoming, slot)
        sent_down = shifted(grad_in, "section", -1)
        grad_store = jnp.where(
            active, lax.dynamic_update_index_in_dim(grad_store, grad_in, slot, 0), grad_store
        )
        qkv_store = jnp.where(
            active, lax.dynamic_update_index_in_dim(qkv_store, qkv_grad, slot, 0), qkv_store
        )
        incoming_store = jnp.where(
            active,
            lax.dynamic_update_index_in_dim(incoming_store, incoming, slot, 0),
            incoming_store,
        )
        return (sent_down, grad_store, qkv_store, incoming_store)

    initial = (
        jnp.zeros((shard_rows, model_width), jnp.bfloat16),
        jnp.zeros((micro_count, shard_rows, model_width), jnp.bfloat16),
        jnp.zeros((micro_count, shard_rows, 3 * model_width), jnp.bfloat16),
        jnp.zeros((micro_count, shard_rows, model_width), jnp.bfloat16),
    )
    received, grad_store, qkv_store, incoming_store = lax.fori_loop(
        0, sections + micro_count - 1, step, initial
    )
    flat_norm = rounded_norm.reshape(-1, model_width)
    flat_attended = attended.reshape(-1, model_width)
    flat_qkv = qkv_store.reshape(-1, 3 * model_width)
    flat_incoming = incoming_store.reshape(-1, model_width)
    contract = (((0,), (0,)), ((), ()))
    first = lax.dot_general(flat_norm, flat_qkv, contract, preferred_element_type=jnp.float32)
    second = lax.dot_general(
        flat_attended, flat_incoming, contract, preferred_element_type=jnp.float32
    )
    summed = lax.psum_scatter(
        jnp.concatenate([first, second], 1).astype(jnp.bfloat16),
        "tm",
        scatter_dimension=0,
        tiled=True,
    ).astype(jnp.float32)
    return (
        grad_store[None],
        summed[None, :, : 3 * model_width],
        summed[None, :, 3 * model_width :],
    )


def solution(mesh):
    placed = (
        P("section", None, "tm", None),
        P(None, "tm", None),
        P("section", None, None),
        P("section", None, None),
        P("tm", None),
    )
    return jax.shard_map(
        per_device,
        mesh=mesh,
        in_specs=placed,
        out_specs=(
            P("section", None, "tm", None),
            P("section", "tm", None),
            P("section", "tm", None),
        ),
        check_vma=False,
    )
```

profile of v0, /device:TPU:2, one launch (start us, length us, event | category | flops | bytes accessed | tf_op | source)
XLA Modules:
  0.0 832.1 jit_solution(8413737208100853493)
XLA Ops:
  9.4 3.8 convolution_convert_fusion.1
  16.6 78.4 %all-gather.2.cloned.1.call-done = bf16[2,2048,2048]{2,1,0:T(8,128)(2,1)} async-done(((bf16[2,64,2048]{2,1,0:T(8,128)(2,1)}), bf16[2,2048,2048]{2,1,0:T(8,128)(2,1)}) %all-gather.2.cloned.1.call-update) | async-done | bytes 16777232 | tf_op jit(solution)/shard_map/all_gather | solution.py:110
  104.5 3.5 slice_bitcast_fusion.6
  108.0 4.6 copy.45
  132.7 568.1 %while.21 = (s32[]{:T(128)}, bf16[64,1024]{1,0:T(8,128)(2,1)}, bf16[2,64,1024]{2,1,0:T(8,128)(2,1)}, bf16[2,64,3072]{2,1,0:T(8,128)(2,1)}, bf16[2,64,1024]{2,1,0...) while((s32[]{:T(128)}, bf16[64,1024]{1,0:T(8,128)(2,1)}, ...), condition=%wide.region_13.14_spmd, body=%wide.region_5.13_spmd.sunk | while | flops 800390528 | bytes 100328176 | solution.py:196
  139.4 3.3 collective-permute-start.2
  148.2 4.9 collective-permute-done.1
  153.2 5.3 collective-permute-done.3
  166.7 3.7 collective-permute-done.5
  183.3 3.9 collective-permute-done
  187.2 3.8 collective-permute-done.1
  191.0 3.4 collective-permute-done.3
  203.4 3.2 collective-permute-done.5
  220.0 4.4 collective-permute-done
  224.4 3.8 collective-permute-done.1
  239.3 3.6 collective-permute-done.5
  255.9 3.2 collective-permute-done
  259.1 5.5 collective-permute-done.1
  275.9 3.8 collective-permute-done.5
  289.7 3.1 collective-permute-start.4
  292.8 3.3 collective-permute-done
  296.2 5.3 collective-permute-done.1
  312.8 3.2 collective-permute-done.5
  324.0 3.1 collective-permute-start.3
  327.1 3.3 collective-permute-start.4
  330.4 3.9 collective-permute-done
  334.2 5.5 collective-permute-done.1
  348.6 4.8 collective-permute-done.5
  361.5 3.1 collective-permute-start.3
  364.6 3.3 collective-permute-start.4
  367.9 4.0 collective-permute-done
  371.9 5.9 collective-permute-done.1
  385.1 189.5 %collective-permute-done.5 = bf16[64,1024]{1,0:T(8,128)(2,1)} collective-permute-done((bf16[64,1024]{1,0:T(8,128)(2,1)}, bf16[64,1024]{1,0:T(8,128)(2,1)}, u32[]{:S(2)}, u32[]{:S(2)}) %collective-permute-start.5) | collective-permute-done | bytes 131104 | tf_op jit(solution)/shard_map/while/body/eval_jaxpr/ppermute | solution.py:14
  576.3 22.1 %conditional.4 = (bf16[5,64,2048]{2,1,0:T(8,128)(2,1)S(1)}, f32[64,2048]{1,0:T(8,128)}, bf16[64,1024]{1,0:T(8,128)(2,1)S(1)}, bf16[1,64,1024]{2,1,0:T(8,128)(2,1)S(1)}) conditional(s32[]{:T(128)} %convert_element_type.218, () %tuple.93, (s32[]{:T(128)}, bf16[2,384,2048]{1,2,0:T(8,128)(2,1)}, pred[64,384]{1,0:T(8,128)(4,1)}, ...), branch_computations={%region_6.6_spmd, %region_7.9_spmd} | conditional | flops 393805184 | bytes 68079920 | solution.py:169
  606.8 3.3 collective-permute-start.4
  610.1 4.3 collective-permute-done
  614.4 5.5 collective-permute-done.1
  622.9 6.8 conditional.5
  622.9 5.1 fusion
  638.7 22.1 %conditional.4 = (bf16[5,64,2048]{2,1,0:T(8,128)(2,1)S(1)}, f32[64,2048]{1,0:T(8,128)}, bf16[64,1024]{1,0:T(8,128)(2,1)S(1)}, bf16[1,64,1024]{2,1,0:T(8,128)(2,1)S(1)}) conditional(s32[]{:T(128)} %convert_element_type.218, () %tuple.93, (s32[]{:T(128)}, bf16[2,384,2048]{1,2,0:T(8,128)(2,1)}, pred[64,384]{1,0:T(8,128)(4,1)}, ...), branch_computations={%region_6.6_spmd, %region_7.9_spmd} | conditional | flops 393805184 | bytes 68079920 | solution.py:169
  666.1 3.1 collective-permute-start.3
  672.2 7.2 collective-permute-done
  679.5 5.6 collective-permute-done.1
  686.4 6.8 conditional.5
  686.4 5.1 fusion
  700.8 5.9 bitcast_convert_fusion
  708.3 6.9 pad_maximum_fusion.3
  715.2 107.6 %reduce-scatter.2.cloned.1.call-done = bf16[32,4096]{1,0:T(8,128)(2,1)} async-done(((bf16[1024,4096]{1,0:T(8,128)(2,1)}), bf16[32,4096]{1,0:T(8,128)(2,1)}) %reduce-scatter.2.cloned.1.call-update) | async-done | bytes 262160 | tf_op jit(solution)/shard_map/reduce_scatter | solution.py:208
  (369 shorter events, 281.2 us)
Async XLA Ops:
  7.2 87.9 %all-gather.2.cloned.1.call-start = ((), (), s32[]{:S(2)}) async-start(), calls=%async_computation.1 | async-start | bytes 17301504 | tf_op jit(solution)/shard_map/all_gather | solution.py:110
  14.3 808.5 %reduce-scatter.2.cloned.1.call-start = ((), (), s32[]{:S(2)}) async-start(), calls=%async_computation.2 | async-start | bytes 8650752 | tf_op jit(solution)/shard_map/reduce_scatter | solution.py:208
  135.6 12.6 %collective-permute-start = (bf16[64,2048]{1,0:T(8,128)(2,1)S(1)}, bf16[64,2048]{1,0:T(8,128)(2,1)S(1)}, u32[]{:S(2)}, u32[]{:S(2)}) collective-permute-start(bf16[64,2048]{1,0:T(8,128)(2,1)S(1)} %get-tuple-element.614), channel_id=1, source_target_pairs={{16,0},{17,1},{18,2},{19,3},{20,4},{21,5},{22,6},{23,7},{24,8},{25... | collective-permute-start | bytes 786440 | tf_op jit(solution)/shard_map/while/body/eval_jaxpr/ppermute | solution.py:14
  136.9 16.2 %collective-permute-start.1 = (bf16[64,2048]{1,0:T(8,128)(2,1)S(1)}, bf16[64,2048]{1,0:T(8,128)(2,1)S(1)}, u32[]{:S(2)}, u32[]{:S(2)}) collective-permute-start(bf16[64,2048]{1,0:T(8,128)(2,1)S(1)} %get-tuple-element.615), channel_id=1, source_target_pairs={{8,0},{9,1},{10,2},{11,3},{12,4},{13,5},{14,6},{15,7},{16,8},{17,9... | collective-permute-start | bytes 786440 | tf_op jit(solution)/shard_map/while/body/eval_jaxpr/ppermute | solution.py:14
  139.4 13.8 %collective-permute-start.2 = (bf16[64,2048]{1,0:T(8,128)(2,1)S(1)}, bf16[64,2048]{1,0:T(8,128)(2,1)S(1)}, u32[]{:S(2)}, u32[]{:S(2)}) collective-permute-start(bf16[64,2048]{1,0:T(8,128)(2,1)S(1)} %get-tuple-element.616), channel_id=1, source_target_pairs={{4,0},{5,1},{6,2},{7,3},{8,4},{9,5},{10,6},{11,7},{12,8},{13,9},{1... | collective-permute-start | bytes 786440 | tf_op jit(solution)/shard_map/while/body/eval_jaxpr/ppermute | solution.py:14
  142.7 15.7 %collective-permute-start.3 = (bf16[64,2048]{1,0:T(8,128)(2,1)S(1)}, bf16[64,2048]{1,0:T(8,128)(2,1)S(1)}, u32[]{:S(2)}, u32[]{:S(2)}) collective-permute-start(bf16[64,2048]{1,0:T(8,128)(2,1)S(1)} %get-tuple-element.617), channel_id=1, source_target_pairs={{2,0},{3,1},{4,2},{5,3},{6,4},{7,5},{8,6},{9,7},{10,8},{11,9},{12,... | collective-permute-start | bytes 786440 | tf_op jit(solution)/shard_map/while/body/eval_jaxpr/ppermute | solution.py:14
  145.8 14.2 %collective-permute-start.4 = (bf16[64,2048]{1,0:T(8,128)(2,1)S(1)}, bf16[64,2048]{1,0:T(8,128)(2,1)S(1)}, u32[]{:S(2)}, u32[]{:S(2)}) collective-permute-start(bf16[64,2048]{1,0:T(8,128)(2,1)S(1)} %get-tuple-element.619), channel_id=1, source_target_pairs={{1,0},{2,1},{3,2},{4,3},{5,4},{6,5},{7,6},{8,7},{9,8},{10,9},{11,1... | collective-permute-start | bytes 786440 | tf_op jit(solution)/shard_map/while/body/eval_jaxpr/ppermute | solution.py:14
  173.3 13.9 %collective-permute-start = (bf16[64,2048]{1,0:T(8,128)(2,1)S(1)}, bf16[64,2048]{1,0:T(8,128)(2,1)S(1)}, u32[]{:S(2)}, u32[]{:S(2)}) collective-permute-start(bf16[64,2048]{1,0:T(8,128)(2,1)S(1)} %get-tuple-element.614), channel_id=1, source_target_pairs={{16,0},{17,1},{18,2},{19,3},{20,4},{21,5},{22,6},{23,7},{24,8},{25... | collective-permute-start | bytes 786440 | tf_op jit(solution)/shard_map/while/body/eval_jaxpr/ppermute | solution.py:14
  174.6 16.4 %collective-permute-start.1 = (bf16[64,2048]{1,0:T(8,128)(2,1)S(1)}, bf16[64,2048]{1,0:T(8,128)(2,1)S(1)}, u32[]{:S(2)}, u32[]{:S(2)}) collective-permute-start(bf16[64,2048]{1,0:T(8,128)(2,1)S(1)} %get-tuple-element.615), channel_id=1, source_target_pairs={{8,0},{9,1},{10,2},{11,3},{12,4},{13,5},{14,6},{15,7},{16,8},{17,9... | collective-permute-start | bytes 786440 | tf_op jit(solution)/shard_map/while/body/eval_jaxpr/ppermute | solution.py:14
  176.5 14.4 %collective-permute-start.2 = (bf16[64,2048]{1,0:T(8,128)(2,1)S(1)}, bf16[64,2048]{1,0:T(8,128)(2,1)S(1)}, u32[]{:S(2)}, u32[]{:S(2)}) collective-permute-start(bf16[64,2048]{1,0:T(8,128)(2,1)S(1)} %get-tuple-element.616), channel_id=1, source_target_pairs={{4,0},{5,1},{6,2},{7,3},{8,4},{9,5},{10,6},{11,7},{12,8},{13,9},{1... | collective-permute-start | bytes 786440 | tf_op jit(solution)/shard_map/while/body/eval_jaxpr/ppermute | solution.py:14
  178.5 16.0 %collective-permute-start.3 = (bf16[64,2048]{1,0:T(8,128)(2,1)S(1)}, bf16[64,2048]{1,0:T(8,128)(2,1)S(1)}, u32[]{:S(2)}, u32[]{:S(2)}) collective-permute-start(bf16[64,2048]{1,0:T(8,128)(2,1)S(1)} %get-tuple-element.617), channel_id=1, source_target_pairs={{2,0},{3,1},{4,2},{5,3},{6,4},{7,5},{8,6},{9,7},{10,8},{11,9},{12,... | collective-permute-start | bytes 786440 | tf_op jit(solution)/shard_map/while/body/eval_jaxpr/ppermute | solution.py:14
  180.4 16.3 %collective-permute-start.4 = (bf16[64,2048]{1,0:T(8,128)(2,1)S(1)}, bf16[64,2048]{1,0:T(8,128)(2,1)S(1)}, u32[]{:S(2)}, u32[]{:S(2)}) collective-permute-start(bf16[64,2048]{1,0:T(8,128)(2,1)S(1)} %get-tuple-element.619), channel_id=1, source_target_pairs={{1,0},{2,1},{3,2},{4,3},{5,4},{6,5},{7,6},{8,7},{9,8},{10,9},{11,1... | collective-permute-start | bytes 786440 | tf_op jit(solution)/shard_map/while/body/eval_jaxpr/ppermute | solution.py:14
  209.5 14.9 %collective-permute-start = (bf16[64,2048]{1,0:T(8,128)(2,1)S(1)}, bf16[64,2048]{1,0:T(8,128)(2,1)S(1)}, u32[]{:S(2)}, u32[]{:S(2)}) collective-permute-start(bf16[64,2048]{1,0:T(8,128)(2,1)S(1)} %get-tuple-element.614), channel_id=1, source_target_pairs={{16,0},{17,1},{18,2},{19,3},{20,4},{21,5},{22,6},{23,7},{24,8},{25... | collective-permute-start | bytes 786440 | tf_op jit(solution)/shard_map/while/body/eval_jaxpr/ppermute | solution.py:14
  210.8 17.4 %collective-permute-start.1 = (bf16[64,2048]{1,0:T(8,128)(2,1)S(1)}, bf16[64,2048]{1,0:T(8,128)(2,1)S(1)}, u32[]{:S(2)}, u32[]{:S(2)}) collective-permute-start(bf16[64,2048]{1,0:T(8,128)(2,1)S(1)} %get-tuple-element.615), channel_id=1, source_target_pairs={{8,0},{9,1},{10,2},{11,3},{12,4},{13,5},{14,6},{15,7},{16,8},{17,9... | collective-permute-start | bytes 786440 | tf_op jit(solution)/shard_map/while/body/eval_jaxpr/ppermute | solution.py:14
  212.8 15.5 %collective-permute-start.2 = (bf16[64,2048]{1,0:T(8,128)(2,1)S(1)}, bf16[64,2048]{1,0:T(8,128)(2,1)S(1)}, u32[]{:S(2)}, u32[]{:S(2)}) collective-permute-start(bf16[64,2048]{1,0:T(8,128)(2,1)S(1)} %get-tuple-element.616), channel_id=1, source_target_pairs={{4,0},{5,1},{6,2},{7,3},{8,4},{9,5},{10,6},{11,7},{12,8},{13,9},{1... | collective-permute-start | bytes 786440 | tf_op jit(solution)/shard_map/while/body/eval_jaxpr/ppermute | solution.py:14
  214.7 15.0 %collective-permute-start.3 = (bf16[64,2048]{1,0:T(8,128)(2,1)S(1)}, bf16[64,2048]{1,0:T(8,128)(2,1)S(1)}, u32[]{:S(2)}, u32[]{:S(2)}) collective-permute-start(bf16[64,2048]{1,0:T(8,128)(2,1)S(1)} %get-tuple-element.617), channel_id=1, source_target_pairs={{2,0},{3,1},{4,2},{5,3},{6,4},{7,5},{8,6},{9,7},{10,8},{11,9},{12,... | collective-permute-start | bytes 786440 | tf_op jit(solution)/shard_map/while/body/eval_jaxpr/ppermute | solution.py:14
  217.0 15.6 %collective-permute-start.4 = (bf16[64,2048]{1,0:T(8,128)(2,1)S(1)}, bf16[64,2048]{1,0:T(8,128)(2,1)S(1)}, u32[]{:S(2)}, u32[]{:S(2)}) collective-permute-start(bf16[64,2048]{1,0:T(8,128)(2,1)S(1)} %get-tuple-element.619), channel_id=1, source_target_pairs={{1,0},{2,1},{3,2},{4,3},{5,4},{6,5},{7,6},{8,7},{9,8},{10,9},{11,1... | collective-permute-start | bytes 786440 | tf_op jit(solution)/shard_map/while/body/eval_jaxpr/ppermute | solution.py:14
  245.8 13.3 %collective-permute-start = (bf16[64,2048]{1,0:T(8,128)(2,1)S(1)}, bf16[64,2048]{1,0:T(8,128)(2,1)S(1)}, u32[]{:S(2)}, u32[]{:S(2)}) collective-permute-start(bf16[64,2048]{1,0:T(8,128)(2,1)S(1)} %get-tuple-element.614), channel_id=1, source_target_pairs={{16,0},{17,1},{18,2},{19,3},{20,4},{21,5},{22,6},{23,7},{24,8},{25... | collective-permute-start | bytes 786440 | tf_op jit(solution)/shard_map/while/body/eval_jaxpr/ppermute | solution.py:14
  247.1 17.5 %collective-permute-start.1 = (bf16[64,2048]{1,0:T(8,128)(2,1)S(1)}, bf16[64,2048]{1,0:T(8,128)(2,1)S(1)}, u32[]{:S(2)}, u32[]{:S(2)}) collective-permute-start(bf16[64,2048]{1,0:T(8,128)(2,1)S(1)} %get-tuple-element.615), channel_id=1, source_target_pairs={{8,0},{9,1},{10,2},{11,3},{12,4},{13,5},{14,6},{15,7},{16,8},{17,9... | collective-permute-start | bytes 786440 | tf_op jit(solution)/shard_map/while/body/eval_jaxpr/ppermute | solution.py:14
  249.0 15.6 %collective-permute-start.2 = (bf16[64,2048]{1,0:T(8,128)(2,1)S(1)}, bf16[64,2048]{1,0:T(8,128)(2,1)S(1)}, u32[]{:S(2)}, u32[]{:S(2)}) collective-permute-start(bf16[64,2048]{1,0:T(8,128)(2,1)S(1)} %get-tuple-element.616), channel_id=1, source_target_pairs={{4,0},{5,1},{6,2},{7,3},{8,4},{9,5},{10,6},{11,7},{12,8},{13,9},{1... | collective-permute-start | bytes 786440 | tf_op jit(solution)/shard_map/while/body/eval_jaxpr/ppermute | solution.py:14
  250.9 15.4 %collective-permute-start.3 = (bf16[64,2048]{1,0:T(8,128)(2,1)S(1)}, bf16[64,2048]{1,0:T(8,128)(2,1)S(1)}, u32[]{:S(2)}, u32[]{:S(2)}) collective-permute-start(bf16[64,2048]{1,0:T(8,128)(2,1)S(1)} %get-tuple-element.617), channel_id=1, source_target_pairs={{2,0},{3,1},{4,2},{5,3},{6,4},{7,5},{8,6},{9,7},{10,8},{11,9},{12,... | collective-permute-start | bytes 786440 | tf_op jit(solution)/shard_map/while/body/eval_jaxpr/ppermute | solution.py:14
  252.9 16.3 %collective-permute-start.4 = (bf16[64,2048]{1,0:T(8,128)(2,1)S(1)}, bf16[64,2048]{1,0:T(8,128)(2,1)S(1)}, u32[]{:S(2)}, u32[]{:S(2)}) collective-permute-start(bf16[64,2048]{1,0:T(8,128)(2,1)S(1)} %get-tuple-element.619), channel_id=1, source_target_pairs={{1,0},{2,1},{3,2},{4,3},{5,4},{6,5},{7,6},{8,7},{9,8},{10,9},{11,1... | collective-permute-start | bytes 786440 | tf_op jit(solution)/shard_map/while/body/eval_jaxpr/ppermute | solution.py:14
  282.6 13.5 %collective-permute-start = (bf16[64,2048]{1,0:T(8,128)(2,1)S(1)}, bf16[64,2048]{1,0:T(8,128)(2,1)S(1)}, u32[]{:S(2)}, u32[]{:S(2)}) collective-permute-start(bf16[64,2048]{1,0:T(8,128)(2,1)S(1)} %get-tuple-element.614), channel_id=1, source_target_pairs={{16,0},{17,1},{18,2},{19,3},{20,4},{21,5},{22,6},{23,7},{24,8},{25... | collective-permute-start | bytes 786440 | tf_op jit(solution)/shard_map/while/body/eval_jaxpr/ppermute | solution.py:14
  283.9 17.5 %collective-permute-start.1 = (bf16[64,2048]{1,0:T(8,128)(2,1)S(1)}, bf16[64,2048]{1,0:T(8,128)(2,1)S(1)}, u32[]{:S(2)}, u32[]{:S(2)}) collective-permute-start(bf16[64,2048]{1,0:T(8,128)(2,1)S(1)} %get-tuple-element.615), channel_id=1, source_target_pairs={{8,0},{9,1},{10,2},{11,3},{12,4},{13,5},{14,6},{15,7},{16,8},{17,9... | collective-permute-start | bytes 786440 | tf_op jit(solution)/shard_map/while/body/eval_jaxpr/ppermute | solution.py:14
  285.9 15.6 %collective-permute-start.2 = (bf16[64,2048]{1,0:T(8,128)(2,1)S(1)}, bf16[64,2048]{1,0:T(8,128)(2,1)S(1)}, u32[]{:S(2)}, u32[]{:S(2)}) collective-permute-start(bf16[64,2048]{1,0:T(8,128)(2,1)S(1)} %get-tuple-element.616), channel_id=1, source_target_pairs={{4,0},{5,1},{6,2},{7,3},{8,4},{9,5},{10,6},{11,7},{12,8},{13,9},{1... | collective-permute-start | bytes 786440 | tf_op jit(solution)/shard_map/while/body/eval_jaxpr/ppermute | solution.py:14
  287.8 15.4 %collective-permute-start.3 = (bf16[64,2048]{1,0:T(8,128)(2,1)S(1)}, bf16[64,2048]{1,0:T(8,128)(2,1)S(1)}, u32[]{:S(2)}, u32[]{:S(2)}) collective-permute-start(bf16[64,2048]{1,0:T(8,128)(2,1)S(1)} %get-tuple-element.617), channel_id=1, source_target_pairs={{2,0},{3,1},{4,2},{5,3},{6,4},{7,5},{8,6},{9,7},{10,8},{11,9},{12,... | collective-permute-start | bytes 786440 | tf_op jit(solution)/shard_map/while/body/eval_jaxpr/ppermute | solution.py:14
  289.7 16.3 %collective-permute-start.4 = (bf16[64,2048]{1,0:T(8,128)(2,1)S(1)}, bf16[64,2048]{1,0:T(8,128)(2,1)S(1)}, u32[]{:S(2)}, u32[]{:S(2)}) collective-permute-start(bf16[64,2048]{1,0:T(8,128)(2,1)S(1)} %get-tuple-element.619), channel_id=1, source_target_pairs={{1,0},{2,1},{3,2},{4,3},{5,4},{6,5},{7,6},{8,7},{9,8},{10,9},{11,1... | collective-permute-start | bytes 786440 | tf_op jit(solution)/shard_map/while/body/eval_jaxpr/ppermute | solution.py:14
  318.9 15.4 %collective-permute-start = (bf16[64,2048]{1,0:T(8,128)(2,1)S(1)}, bf16[64,2048]{1,0:T(8,128)(2,1)S(1)}, u32[]{:S(2)}, u32[]{:S(2)}) collective-permute-start(bf16[64,2048]{1,0:T(8,128)(2,1)S(1)} %get-tuple-element.614), channel_id=1, source_target_pairs={{16,0},{17,1},{18,2},{19,3},{20,4},{21,5},{22,6},{23,7},{24,8},{25... | collective-permute-start | bytes 786440 | tf_op jit(solution)/shard_map/while/body/eval_jaxpr/ppermute | solution.py:14
  320.2 19.5 %collective-permute-start.1 = (bf16[64,2048]{1,0:T(8,128)(2,1)S(1)}, bf16[64,2048]{1,0:T(8,128)(2,1)S(1)}, u32[]{:S(2)}, u32[]{:S(2)}) collective-permute-start(bf16[64,2048]{1,0:T(8,128)(2,1)S(1)} %get-tuple-element.615), channel_id=1, source_target_pairs={{8,0},{9,1},{10,2},{11,3},{12,4},{13,5},{14,6},{15,7},{16,8},{17,9... | collective-permute-start | bytes 786440 | tf_op jit(solution)/shard_map/while/body/eval_jaxpr/ppermute | solution.py:14
  322.1 17.6 %collective-permute-start.2 = (bf16[64,2048]{1,0:T(8,128)(2,1)S(1)}, bf16[64,2048]{1,0:T(8,128)(2,1)S(1)}, u32[]{:S(2)}, u32[]{:S(2)}) collective-permute-start(bf16[64,2048]{1,0:T(8,128)(2,1)S(1)} %get-tuple-element.616), channel_id=1, source_target_pairs={{4,0},{5,1},{6,2},{7,3},{8,4},{9,5},{10,6},{11,7},{12,8},{13,9},{1... | collective-permute-start | bytes 786440 | tf_op jit(solution)/shard_map/while/body/eval_jaxpr/ppermute | solution.py:14
  324.0 15.7 %collective-permute-start.3 = (bf16[64,2048]{1,0:T(8,128)(2,1)S(1)}, bf16[64,2048]{1,0:T(8,128)(2,1)S(1)}, u32[]{:S(2)}, u32[]{:S(2)}) collective-permute-start(bf16[64,2048]{1,0:T(8,128)(2,1)S(1)} %get-tuple-element.617), channel_id=1, source_target_pairs={{2,0},{3,1},{4,2},{5,3},{6,4},{7,5},{8,6},{9,7},{10,8},{11,9},{12,... | collective-permute-start | bytes 786440 | tf_op jit(solution)/shard_map/while/body/eval_jaxpr/ppermute | solution.py:14
  327.1 14.8 %collective-permute-start.4 = (bf16[64,2048]{1,0:T(8,128)(2,1)S(1)}, bf16[64,2048]{1,0:T(8,128)(2,1)S(1)}, u32[]{:S(2)}, u32[]{:S(2)}) collective-permute-start(bf16[64,2048]{1,0:T(8,128)(2,1)S(1)} %get-tuple-element.619), channel_id=1, source_target_pairs={{1,0},{2,1},{3,2},{4,3},{5,4},{6,5},{7,6},{8,7},{9,8},{10,9},{11,1... | collective-permute-start | bytes 786440 | tf_op jit(solution)/shard_map/while/body/eval_jaxpr/ppermute | solution.py:14
  356.4 15.5 %collective-permute-start = (bf16[64,2048]{1,0:T(8,128)(2,1)S(1)}, bf16[64,2048]{1,0:T(8,128)(2,1)S(1)}, u32[]{:S(2)}, u32[]{:S(2)}) collective-permute-start(bf16[64,2048]{1,0:T(8,128)(2,1)S(1)} %get-tuple-element.614), channel_id=1, source_target_pairs={{16,0},{17,1},{18,2},{19,3},{20,4},{21,5},{22,6},{23,7},{24,8},{25... | collective-permute-start | bytes 786440 | tf_op jit(solution)/shard_map/while/body/eval_jaxpr/ppermute | solution.py:14
  357.7 20.1 %collective-permute-start.1 = (bf16[64,2048]{1,0:T(8,128)(2,1)S(1)}, bf16[64,2048]{1,0:T(8,128)(2,1)S(1)}, u32[]{:S(2)}, u32[]{:S(2)}) collective-permute-start(bf16[64,2048]{1,0:T(8,128)(2,1)S(1)} %get-tuple-element.615), channel_id=1, source_target_pairs={{8,0},{9,1},{10,2},{11,3},{12,4},{13,5},{14,6},{15,7},{16,8},{17,9... | collective-permute-start | bytes 786440 | tf_op jit(solution)/shard_map/while/body/eval_jaxpr/ppermute | solution.py:14
  359.6 18.2 %collective-permute-start.2 = (bf16[64,2048]{1,0:T(8,128)(2,1)S(1)}, bf16[64,2048]{1,0:T(8,128)(2,1)S(1)}, u32[]{:S(2)}, u32[]{:S(2)}) collective-permute-start(bf16[64,2048]{1,0:T(8,128)(2,1)S(1)} %get-tuple-element.616), channel_id=1, source_target_pairs={{4,0},{5,1},{6,2},{7,3},{8,4},{9,5},{10,6},{11,7},{12,8},{13,9},{1... | collective-permute-start | bytes 786440 | tf_op jit(solution)/shard_map/while/body/eval_jaxpr/ppermute | solution.py:14
  361.5 16.3 %collective-permute-start.3 = (bf16[64,2048]{1,0:T(8,128)(2,1)S(1)}, bf16[64,2048]{1,0:T(8,128)(2,1)S(1)}, u32[]{:S(2)}, u32[]{:S(2)}) collective-permute-start(bf16[64,2048]{1,0:T(8,128)(2,1)S(1)} %get-tuple-element.617), channel_id=1, source_target_pairs={{2,0},{3,1},{4,2},{5,3},{6,4},{7,5},{8,6},{9,7},{10,8},{11,9},{12,... | collective-permute-start | bytes 786440 | tf_op jit(solution)/shard_map/while/body/eval_jaxpr/ppermute | solution.py:14
  364.6 13.7 %collective-permute-start.4 = (bf16[64,2048]{1,0:T(8,128)(2,1)S(1)}, bf16[64,2048]{1,0:T(8,128)(2,1)S(1)}, u32[]{:S(2)}, u32[]{:S(2)}) collective-permute-start(bf16[64,2048]{1,0:T(8,128)(2,1)S(1)} %get-tuple-element.619), channel_id=1, source_target_pairs={{1,0},{2,1},{3,2},{4,3},{5,4},{6,5},{7,6},{8,7},{9,8},{10,9},{11,1... | collective-permute-start | bytes 786440 | tf_op jit(solution)/shard_map/while/body/eval_jaxpr/ppermute | solution.py:14
  380.3 194.2 %collective-permute-start.5 = (bf16[64,1024]{1,0:T(8,128)(2,1)}, bf16[64,1024]{1,0:T(8,128)(2,1)}, u32[]{:S(2)}, u32[]{:S(2)}) collective-permute-start(bf16[64,1024]{1,0:T(8,128)(2,1)} %get-tuple-element.621), channel_id=1, source_target_pairs={{32,0},{64,32},{96,64},{128,96},{160,128},{192,160},{224,192},{33,... | collective-permute-start | bytes 393224 | tf_op jit(solution)/shard_map/while/body/eval_jaxpr/ppermute | solution.py:14
  598.6 15.8 %collective-permute-start = (bf16[64,2048]{1,0:T(8,128)(2,1)S(1)}, bf16[64,2048]{1,0:T(8,128)(2,1)S(1)}, u32[]{:S(2)}, u32[]{:S(2)}) collective-permute-start(bf16[64,2048]{1,0:T(8,128)(2,1)S(1)} %get-tuple-element.614), channel_id=1, source_target_pairs={{16,0},{17,1},{18,2},{19,3},{20,4},{21,5},{22,6},{23,7},{24,8},{25... | collective-permute-start | bytes 786440 | tf_op jit(solution)/shard_map/while/body/eval_jaxpr/ppermute | solution.py:14
  599.9 20.0 %collective-permute-start.1 = (bf16[64,2048]{1,0:T(8,128)(2,1)S(1)}, bf16[64,2048]{1,0:T(8,128)(2,1)S(1)}, u32[]{:S(2)}, u32[]{:S(2)}) collective-permute-start(bf16[64,2048]{1,0:T(8,128)(2,1)S(1)} %get-tuple-element.615), channel_id=1, source_target_pairs={{8,0},{9,1},{10,2},{11,3},{12,4},{13,5},{14,6},{15,7},{16,8},{17,9... | collective-permute-start | bytes 786440 | tf_op jit(solution)/shard_map/while/body/eval_jaxpr/ppermute | solution.py:14
  601.8 18.1 %collective-permute-start.2 = (bf16[64,2048]{1,0:T(8,128)(2,1)S(1)}, bf16[64,2048]{1,0:T(8,128)(2,1)S(1)}, u32[]{:S(2)}, u32[]{:S(2)}) collective-permute-start(bf16[64,2048]{1,0:T(8,128)(2,1)S(1)} %get-tuple-element.616), channel_id=1, source_target_pairs={{4,0},{5,1},{6,2},{7,3},{8,4},{9,5},{10,6},{11,7},{12,8},{13,9},{1... | collective-permute-start | bytes 786440 | tf_op jit(solution)/shard_map/while/body/eval_jaxpr/ppermute | solution.py:14
  603.7 16.2 %collective-permute-start.3 = (bf16[64,2048]{1,0:T(8,128)(2,1)S(1)}, bf16[64,2048]{1,0:T(8,128)(2,1)S(1)}, u32[]{:S(2)}, u32[]{:S(2)}) collective-permute-start(bf16[64,2048]{1,0:T(8,128)(2,1)S(1)} %get-tuple-element.617), channel_id=1, source_target_pairs={{2,0},{3,1},{4,2},{5,3},{6,4},{7,5},{8,6},{9,7},{10,8},{11,9},{12,... | collective-permute-start | bytes 786440 | tf_op jit(solution)/shard_map/while/body/eval_jaxpr/ppermute | solution.py:14
  606.8 14.8 %collective-permute-start.4 = (bf16[64,2048]{1,0:T(8,128)(2,1)S(1)}, bf16[64,2048]{1,0:T(8,128)(2,1)S(1)}, u32[]{:S(2)}, u32[]{:S(2)}) collective-permute-start(bf16[64,2048]{1,0:T(8,128)(2,1)S(1)} %get-tuple-element.619), channel_id=1, source_target_pairs={{1,0},{2,1},{3,2},{4,3},{5,4},{6,5},{7,6},{8,7},{9,8},{10,9},{11,1... | collective-permute-start | bytes 786440 | tf_op jit(solution)/shard_map/while/body/eval_jaxpr/ppermute | solution.py:14
  660.9 18.5 %collective-permute-start = (bf16[64,2048]{1,0:T(8,128)(2,1)S(1)}, bf16[64,2048]{1,0:T(8,128)(2,1)S(1)}, u32[]{:S(2)}, u32[]{:S(2)}) collective-permute-start(bf16[64,2048]{1,0:T(8,128)(2,1)S(1)} %get-tuple-element.614), channel_id=1, source_target_pairs={{16,0},{17,1},{18,2},{19,3},{20,4},{21,5},{22,6},{23,7},{24,8},{25... | collective-permute-start | bytes 786440 | tf_op jit(solution)/shard_map/while/body/eval_jaxpr/ppermute | solution.py:14
  662.2 22.8 %collective-permute-start.1 = (bf16[64,2048]{1,0:T(8,128)(2,1)S(1)}, bf16[64,2048]{1,0:T(8,128)(2,1)S(1)}, u32[]{:S(2)}, u32[]{:S(2)}) collective-permute-start(bf16[64,2048]{1,0:T(8,128)(2,1)S(1)} %get-tuple-element.615), channel_id=1, source_target_pairs={{8,0},{9,1},{10,2},{11,3},{12,4},{13,5},{14,6},{15,7},{16,8},{17,9... | collective-permute-start | bytes 786440 | tf_op jit(solution)/shard_map/while/body/eval_jaxpr/ppermute | solution.py:14
  664.2 20.9 %collective-permute-start.2 = (bf16[64,2048]{1,0:T(8,128)(2,1)S(1)}, bf16[64,2048]{1,0:T(8,128)(2,1)S(1)}, u32[]{:S(2)}, u32[]{:S(2)}) collective-permute-start(bf16[64,2048]{1,0:T(8,128)(2,1)S(1)} %get-tuple-element.616), channel_id=1, source_target_pairs={{4,0},{5,1},{6,2},{7,3},{8,4},{9,5},{10,6},{11,7},{12,8},{13,9},{1... | collective-permute-start | bytes 786440 | tf_op jit(solution)/shard_map/while/body/eval_jaxpr/ppermute | solution.py:14
  666.1 19.0 %collective-permute-start.3 = (bf16[64,2048]{1,0:T(8,128)(2,1)S(1)}, bf16[64,2048]{1,0:T(8,128)(2,1)S(1)}, u32[]{:S(2)}, u32[]{:S(2)}) collective-permute-start(bf16[64,2048]{1,0:T(8,128)(2,1)S(1)} %get-tuple-element.617), channel_id=1, source_target_pairs={{2,0},{3,1},{4,2},{5,3},{6,4},{7,5},{8,6},{9,7},{10,8},{11,9},{12,... | collective-permute-start | bytes 786440 | tf_op jit(solution)/shard_map/while/body/eval_jaxpr/ppermute | solution.py:14
  669.2 15.9 %collective-permute-start.4 = (bf16[64,2048]{1,0:T(8,128)(2,1)S(1)}, bf16[64,2048]{1,0:T(8,128)(2,1)S(1)}, u32[]{:S(2)}, u32[]{:S(2)}) collective-permute-start(bf16[64,2048]{1,0:T(8,128)(2,1)S(1)} %get-tuple-element.619), channel_id=1, source_target_pairs={{1,0},{2,1},{3,2},{4,3},{5,4},{6,5},{7,6},{8,7},{9,8},{10,9},{11,1... | collective-permute-start | bytes 786440 | tf_op jit(solution)/shard_map/while/body/eval_jaxpr/ppermute | solution.py:14
  (45 other events, 416.6 us)
Sparse Core Ops, SparseCore 0:
  14.5 80.5 all-gather.1
  715.3 107.4 reduce-scatter.1
where the time goes:
time: 836 us; the launch traced here: 832 us
  waiting for transfers between devices  514 us (61%)
  starting transfers between devices  110 us (13%)
  local copies, waits for them, and re-layouts  74.5 us (9%)
  other arithmetic  72.8 us (9%)
  matrix products  44.7 us (5%)
  between operations  14.3 us (2%)
    ppermute x54, waiting for transfers between devices, shifted(): lax.ppermute(value, axis, [(source, source + steps) for source in range(i...  328 us
    ppermute x54, starting transfers between devices, shifted(): lax.ppermute(value, axis, [(source, source + steps) for source in range(i...  110 us
    reduce_scatter x1, waiting for transfers between devices, per_device(): lax.psum_scatter(jnp.concatenate([first, second], 1).astype(jnp.bfloat16)...  108 us
    all_gather x1, waiting for transfers between devices, per_device(): every_pair = lax.all_gather(pairs, 'tm', axis=1, tiled=True)  78.4 us
    select_n x9, other arithmetic, step(): jnp.where(active, lax.dynamic_update_index_in_dim(qkv_store, qkv_grad, sl...  16.7 us
  transfers between devices with their start and end apart: 56, of which 42 were waited for; matrix products, arithmetic and copies ran while one was open for 4% of the time, Pallas kernels for 0%

commit v1 on v0

--- a/solution.py
+++ b/solution.py
@@ -107,7 +107,16 @@
     qkv = jnp.dot(rounded_norm.reshape(-1, model_width), w_qkv, preferred_element_type=jnp.float32)
     qkv = qkv.astype(jnp.bfloat16).reshape(micro_count, shard_rows, 3 * model_width)
     pairs = qkv[..., model_width:]
-    every_pair = lax.all_gather(pairs, "tm", axis=1, tiled=True)
+    _connect_stacks_all = lambda vector, chip_axis, which_dim: jnp.concatenate(
+        lax.all_to_all(
+            jnp.stack([vector] * lax.axis_size(chip_axis)),
+            axis_name=chip_axis,
+            split_axis=0,
+            concat_axis=0,
+        ),
+        axis=which_dim,
+    )
+    every_pair = _connect_stacks_all(pairs, "tm", 1)
     shard_index = lax.axis_index("tm")
     far_list = []
     for level in range(levels):

time: 836 us -> 1040 us (1.24)
  waiting for transfers between devices: 514 us -> 659 us
  starting transfers between devices: 110 us -> 163 us
    all_to_all x0 -> x1, waiting for transfers between devices: none -> 222 us  [per_device(): lax.all_to_all(jnp.stack([vector] * lax.axis_size(chip_axis)), axis_name=...]
    all_gather x1 -> x0, waiting for transfers between devices: 78.4 us -> none  [per_device(): every_pair = lax.all_gather(pairs, 'tm', axis=1, tiled=True)]
    ppermute x54, starting transfers between devices: 110 us -> 155 us  [shifted(): lax.ppermute(value, axis, [(source, source + steps) for source in range(i...]
  transfers between devices with their start and end apart: 56 -> 56, of which waited for: 42 -> 41; matrix products, arithmetic and copies ran while one was open for 4% -> 3% of each run, Pallas kernels for 0% -> 0%
where the time goes in v1:
time: 1040 us
  waiting for transfers between devices  659 us (63%)
  starting transfers between devices  163 us (16%)
  local copies, waits for them, and re-layouts  81 us (8%)
  other arithmetic  72.4 us (7%)
  matrix products  43.9 us (4%)
  between operations  14.3 us (1%)
    ppermute x54, waiting for transfers between devices, shifted(): lax.ppermute(value, axis, [(source, source + steps) for source in range(i...  328 us
    all_to_all x1, waiting for transfers between devices, per_device(): lax.all_to_all(jnp.stack([vector] * lax.axis_size(chip_axis)), axis_name=...  222 us
    ppermute x54, starting transfers between devices, shifted(): lax.ppermute(value, axis, [(source, source + steps) for source in range(i...  155 us
    reduce_scatter x1, waiting for transfers between devices, per_device(): lax.psum_scatter(jnp.concatenate([first, second], 1).astype(jnp.bfloat16)...  109 us
  transfers between devices with their start and end apart: 56, of which 41 were waited for; matrix products, arithmetic and copies ran while one was open for 3% of the time, Pallas kernels for 0%

profile of v1, /device:TPU:2, one launch (start us, length us, event | category | flops | bytes accessed | tf_op | source)
XLA Modules:
  0.0 1035.7 jit_solution(6617794576744270416)
XLA Ops:
  9.3 3.8 convolution_convert_fusion.1
  14.1 6.0 stack.4
  20.1 7.8 all-to-all-start
  30.4 222.0 %all-to-all-done = bf16[32,2,64,2048]{3,2,1,0:T(8,128)(2,1)} async-done(((bf16[32,2,64,2048]{3,2,1,0:T(8,128)(2,1)}), bf16[32,2,64,2048]{3,2,1,0:T(8,128)(2,1)}, u32[]{:S(2)}, u32[]{:S(2)}) %all-to-all-start) | async-done | bytes 16777248 | tf_op jit(solution)/shard_map/all_to_all | solution.py:111
  252.4 8.1 copy.77
  269.1 3.1 fusion.51
  282.7 620.6 %while.21 = (s32[]{:T(128)}, bf16[64,1024]{1,0:T(8,128)(2,1)}, bf16[2,64,1024]{2,1,0:T(8,128)(2,1)}, bf16[2,64,3072]{2,1,0:T(8,128)(2,1)}, bf16[2,64,1024]{2,1,0...) while((s32[]{:T(128)}, bf16[64,1024]{1,0:T(8,128)(2,1)}, ...), condition=%wide.region_13.14_spmd, body=%wide.region_5.13_spmd.sunk | while | flops 800390528 | bytes 102196128 | solution.py:205
  287.8 18.0 %collective-permute-start.1 = (bf16[64,2048]{1,0:T(8,128)(2,1)S(1)}, bf16[64,2048]{1,0:T(8,128)(2,1)S(1)}, u32[]{:S(2)}, u32[]{:S(2)}) collective-permute-start(bf16[64,2048]{1,0:T(8,128)(2,1)S(1)} %get-tuple-element.647), channel_id=1, source_target_pairs={{8,0},{9,1},{10,2},{11,3},{12,4},{13,5},{14,6},{15,7},{16,8},{17,9... | collective-permute-start | bytes 786440 | tf_op jit(solution)/shard_map/while/body/eval_jaxpr/ppermute | solution.py:14
  307.7 32.9 %collective-permute-start.3 = (bf16[64,2048]{1,0:T(8,128)(2,1)S(1)}, bf16[64,2048]{1,0:T(8,128)(2,1)S(1)}, u32[]{:S(2)}, u32[]{:S(2)}) collective-permute-start(bf16[64,2048]{1,0:T(8,128)(2,1)S(1)} %get-tuple-element.649), channel_id=1, source_target_pairs={{2,0},{3,1},{4,2},{5,3},{6,4},{7,5},{8,6},{9,7},{10,8},{11,9},{12,... | collective-permute-start | bytes 786440 | tf_op jit(solution)/shard_map/while/body/eval_jaxpr/ppermute | solution.py:14
  342.6 7.8 collective-permute-done.3
  374.6 3.2 collective-permute-start.4
  379.3 3.9 collective-permute-done.1
  383.2 3.8 collective-permute-done.3
  396.6 3.2 collective-permute-done.5
  411.1 3.2 collective-permute-start.4
  414.3 4.6 collective-permute-done
  418.8 3.8 collective-permute-done.1
  434.1 3.8 collective-permute-done.5
  453.6 5.6 collective-permute-done.1
  471.7 4.6 collective-permute-done.5
  487.2 3.2 collective-permute-start.4
  492.4 5.8 collective-permute-done.1
  510.1 4.9 collective-permute-done.5
  525.9 3.2 collective-permute-start.4
  529.1 3.0 collective-permute-done
  532.1 5.6 collective-permute-done.1
  548.8 3.6 collective-permute-done.5
  563.9 3.3 collective-permute-start.4
  567.2 4.2 collective-permute-done
  571.3 5.6 collective-permute-done.1
  585.7 189.8 %collective-permute-done.5 = bf16[64,1024]{1,0:T(8,128)(2,1)} collective-permute-done((bf16[64,1024]{1,0:T(8,128)(2,1)}, bf16[64,1024]{1,0:T(8,128)(2,1)}, u32[]{:S(2)}, u32[]{:S(2)}) %collective-permute-start.5) | collective-permute-done | bytes 131104 | tf_op jit(solution)/shard_map/while/body/eval_jaxpr/ppermute | solution.py:14
  777.2 22.2 %conditional.4 = (bf16[5,64,2048]{2,1,0:T(8,128)(2,1)S(1)}, f32[64,2048]{1,0:T(8,128)}, bf16[64,1024]{1,0:T(8,128)(2,1)S(1)}, bf16[1,64,1024]{2,1,0:T(8,128)(2,1)S(1)}) conditional(s32[]{:T(128)} %convert_element_type.218, () %tuple.95, (s32[]{:T(128)}, bf16[2,384,2048]{1,2,0:T(8,128)(2,1)}, pred[64,384]{1,0:T(8,128)(4,1)S(1)}, ...), branch_computations={%region_6.6_spmd, %region_7.9_spmd} | conditional | flops 393805184 | bytes 68178248 | solution.py:178
  805.5 3.1 collective-permute-start.3
  808.6 3.3 collective-permute-start.4
  811.9 4.3 collective-permute-done
  816.2 5.3 collective-permute-done.1
  824.8 6.8 conditional.5
  824.8 5.1 fusion
  840.6 22.2 %conditional.4 = (bf16[5,64,2048]{2,1,0:T(8,128)(2,1)S(1)}, f32[64,2048]{1,0:T(8,128)}, bf16[64,1024]{1,0:T(8,128)(2,1)S(1)}, bf16[1,64,1024]{2,1,0:T(8,128)(2,1)S(1)}) conditional(s32[]{:T(128)} %convert_element_type.218, () %tuple.95, (s32[]{:T(128)}, bf16[2,384,2048]{1,2,0:T(8,128)(2,1)}, pred[64,384]{1,0:T(8,128)(4,1)S(1)}, ...), branch_computations={%region_6.6_spmd, %region_7.9_spmd} | conditional | flops 393805184 | bytes 68178248 | solution.py:178
  869.0 3.1 collective-permute-start.3
  872.1 3.2 collective-permute-start.4
  875.3 6.7 collective-permute-done
  882.0 5.8 collective-permute-done.1
  889.1 6.8 conditional.5
  889.1 5.1 fusion
  903.4 5.9 bitcast_convert_fusion
  910.9 6.9 pad_maximum_fusion.3
  917.8 108.6 %reduce-scatter.2.cloned.1.call-done = bf16[32,4096]{1,0:T(8,128)(2,1)} async-done(((bf16[1024,4096]{1,0:T(8,128)(2,1)}), bf16[32,4096]{1,0:T(8,128)(2,1)}) %reduce-scatter.2.cloned.1.call-update) | async-done | bytes 262160 | tf_op jit(solution)/shard_map/reduce_scatter | solution.py:217
  (476 shorter events, 283.8 us)
Async XLA Ops:
  20.1 232.2 %all-to-all-start = ((bf16[32,2,64,2048]{3,2,1,0:T(8,128)(2,1)}), bf16[32,2,64,2048]{3,2,1,0:T(8,128)(2,1)}, u32[]{:S(2)}, u32[]{:S(2)}) async-start(bf16[32,2,64,2048]{3,2,1,0:T(8,128)(2,1)} %stack.4), calls=%async_computation | async-start | bytes 33554432 | tf_op jit(solution)/shard_map/all_to_all | solution.py:111
  28.0 998.4 %reduce-scatter.2.cloned.1.call-start = ((), (), s32[]{:S(2)}) async-start(), calls=%async_computation.2 | async-start | bytes 8650752 | tf_op jit(solution)/shard_map/reduce_scatter | solution.py:217
  286.4 56.2 %collective-permute-start = (bf16[64,2048]{1,0:T(8,128)(2,1)S(1)}, bf16[64,2048]{1,0:T(8,128)(2,1)S(1)}, u32[]{:S(2)}, u32[]{:S(2)}) collective-permute-start(bf16[64,2048]{1,0:T(8,128)(2,1)S(1)} %get-tuple-element.646), channel_id=1, source_target_pairs={{16,0},{17,1},{18,2},{19,3},{20,4},{21,5},{22,6},{23,7},{24,8},{25... | collective-permute-start | bytes 786440 | tf_op jit(solution)/shard_map/while/body/eval_jaxpr/ppermute | solution.py:14
  287.8 54.8 %collective-permute-start.1 = (bf16[64,2048]{1,0:T(8,128)(2,1)S(1)}, bf16[64,2048]{1,0:T(8,128)(2,1)S(1)}, u32[]{:S(2)}, u32[]{:S(2)}) collective-permute-start(bf16[64,2048]{1,0:T(8,128)(2,1)S(1)} %get-tuple-element.647), channel_id=1, source_target_pairs={{8,0},{9,1},{10,2},{11,3},{12,4},{13,5},{14,6},{15,7},{16,8},{17,9... | collective-permute-start | bytes 786440 | tf_op jit(solution)/shard_map/while/body/eval_jaxpr/ppermute | solution.py:14
  305.8 36.8 %collective-permute-start.2 = (bf16[64,2048]{1,0:T(8,128)(2,1)S(1)}, bf16[64,2048]{1,0:T(8,128)(2,1)S(1)}, u32[]{:S(2)}, u32[]{:S(2)}) collective-permute-start(bf16[64,2048]{1,0:T(8,128)(2,1)S(1)} %get-tuple-element.648), channel_id=1, source_target_pairs={{4,0},{5,1},{6,2},{7,3},{8,4},{9,5},{10,6},{11,7},{12,8},{13,9},{1... | collective-permute-start | bytes 786440 | tf_op jit(solution)/shard_map/while/body/eval_jaxpr/ppermute | solution.py:14
  307.7 42.7 %collective-permute-start.3 = (bf16[64,2048]{1,0:T(8,128)(2,1)S(1)}, bf16[64,2048]{1,0:T(8,128)(2,1)S(1)}, u32[]{:S(2)}, u32[]{:S(2)}) collective-permute-start(bf16[64,2048]{1,0:T(8,128)(2,1)S(1)} %get-tuple-element.649), channel_id=1, source_target_pairs={{2,0},{3,1},{4,2},{5,3},{6,4},{7,5},{8,6},{9,7},{10,8},{11,9},{12,... | collective-permute-start | bytes 786440 | tf_op jit(solution)/shard_map/while/body/eval_jaxpr/ppermute | solution.py:14
  340.7 12.6 %collective-permute-start.4 = (bf16[64,2048]{1,0:T(8,128)(2,1)S(1)}, bf16[64,2048]{1,0:T(8,128)(2,1)S(1)}, u32[]{:S(2)}, u32[]{:S(2)}) collective-permute-start(bf16[64,2048]{1,0:T(8,128)(2,1)S(1)} %get-tuple-element.651), channel_id=1, source_target_pairs={{1,0},{2,1},{3,2},{4,3},{5,4},{6,5},{7,6},{8,7},{9,8},{10,9},{11,1... | collective-permute-start | bytes 786440 | tf_op jit(solution)/shard_map/while/body/eval_jaxpr/ppermute | solution.py:14
  366.6 12.7 %collective-permute-start = (bf16[64,2048]{1,0:T(8,128)(2,1)S(1)}, bf16[64,2048]{1,0:T(8,128)(2,1)S(1)}, u32[]{:S(2)}, u32[]{:S(2)}) collective-permute-start(bf16[64,2048]{1,0:T(8,128)(2,1)S(1)} %get-tuple-element.646), channel_id=1, source_target_pairs={{16,0},{17,1},{18,2},{19,3},{20,4},{21,5},{22,6},{23,7},{24,8},{25... | collective-permute-start | bytes 786440 | tf_op jit(solution)/shard_map/while/body/eval_jaxpr/ppermute | solution.py:14
  368.0 15.2 %collective-permute-start.1 = (bf16[64,2048]{1,0:T(8,128)(2,1)S(1)}, bf16[64,2048]{1,0:T(8,128)(2,1)S(1)}, u32[]{:S(2)}, u32[]{:S(2)}) collective-permute-start(bf16[64,2048]{1,0:T(8,128)(2,1)S(1)} %get-tuple-element.647), channel_id=1, source_target_pairs={{8,0},{9,1},{10,2},{11,3},{12,4},{13,5},{14,6},{15,7},{16,8},{17,9... | collective-permute-start | bytes 786440 | tf_op jit(solution)/shard_map/while/body/eval_jaxpr/ppermute | solution.py:14
  370.0 13.3 %collective-permute-start.2 = (bf16[64,2048]{1,0:T(8,128)(2,1)S(1)}, bf16[64,2048]{1,0:T(8,128)(2,1)S(1)}, u32[]{:S(2)}, u32[]{:S(2)}) collective-permute-start(bf16[64,2048]{1,0:T(8,128)(2,1)S(1)} %get-tuple-element.648), channel_id=1, source_target_pairs={{4,0},{5,1},{6,2},{7,3},{8,4},{9,5},{10,6},{11,7},{12,8},{13,9},{1... | collective-permute-start | bytes 786440 | tf_op jit(solution)/shard_map/while/body/eval_jaxpr/ppermute | solution.py:14
  371.9 15.1 %collective-permute-start.3 = (bf16[64,2048]{1,0:T(8,128)(2,1)S(1)}, bf16[64,2048]{1,0:T(8,128)(2,1)S(1)}, u32[]{:S(2)}, u32[]{:S(2)}) collective-permute-start(bf16[64,2048]{1,0:T(8,128)(2,1)S(1)} %get-tuple-element.649), channel_id=1, source_target_pairs={{2,0},{3,1},{4,2},{5,3},{6,4},{7,5},{8,6},{9,7},{10,8},{11,9},{12,... | collective-permute-start | bytes 786440 | tf_op jit(solution)/shard_map/while/body/eval_jaxpr/ppermute | solution.py:14
  374.6 15.3 %collective-permute-start.4 = (bf16[64,2048]{1,0:T(8,128)(2,1)S(1)}, bf16[64,2048]{1,0:T(8,128)(2,1)S(1)}, u32[]{:S(2)}, u32[]{:S(2)}) collective-permute-start(bf16[64,2048]{1,0:T(8,128)(2,1)S(1)} %get-tuple-element.651), channel_id=1, source_target_pairs={{1,0},{2,1},{3,2},{4,3},{5,4},{6,5},{7,6},{8,7},{9,8},{10,9},{11,1... | collective-permute-start | bytes 786440 | tf_op jit(solution)/shard_map/while/body/eval_jaxpr/ppermute | solution.py:14
  403.4 15.4 %collective-permute-start = (bf16[64,2048]{1,0:T(8,128)(2,1)S(1)}, bf16[64,2048]{1,0:T(8,128)(2,1)S(1)}, u32[]{:S(2)}, u32[]{:S(2)}) collective-permute-start(bf16[64,2048]{1,0:T(8,128)(2,1)S(1)} %get-tuple-element.646), channel_id=1, source_target_pairs={{16,0},{17,1},{18,2},{19,3},{20,4},{21,5},{22,6},{23,7},{24,8},{25... | collective-permute-start | bytes 786440 | tf_op jit(solution)/shard_map/while/body/eval_jaxpr/ppermute | solution.py:14
  404.9 17.7 %collective-permute-start.1 = (bf16[64,2048]{1,0:T(8,128)(2,1)S(1)}, bf16[64,2048]{1,0:T(8,128)(2,1)S(1)}, u32[]{:S(2)}, u32[]{:S(2)}) collective-permute-start(bf16[64,2048]{1,0:T(8,128)(2,1)S(1)} %get-tuple-element.647), channel_id=1, source_target_pairs={{8,0},{9,1},{10,2},{11,3},{12,4},{13,5},{14,6},{15,7},{16,8},{17,9... | collective-permute-start | bytes 786440 | tf_op jit(solution)/shard_map/while/body/eval_jaxpr/ppermute | solution.py:14
  406.8 15.8 %collective-permute-start.2 = (bf16[64,2048]{1,0:T(8,128)(2,1)S(1)}, bf16[64,2048]{1,0:T(8,128)(2,1)S(1)}, u32[]{:S(2)}, u32[]{:S(2)}) collective-permute-start(bf16[64,2048]{1,0:T(8,128)(2,1)S(1)} %get-tuple-element.648), channel_id=1, source_target_pairs={{4,0},{5,1},{6,2},{7,3},{8,4},{9,5},{10,6},{11,7},{12,8},{13,9},{1... | collective-permute-start | bytes 786440 | tf_op jit(solution)/shard_map/while/body/eval_jaxpr/ppermute | solution.py:14
  408.7 16.6 %collective-permute-start.3 = (bf16[64,2048]{1,0:T(8,128)(2,1)S(1)}, bf16[64,2048]{1,0:T(8,128)(2,1)S(1)}, u32[]{:S(2)}, u32[]{:S(2)}) collective-permute-start(bf16[64,2048]{1,0:T(8,128)(2,1)S(1)} %get-tuple-element.649), channel_id=1, source_target_pairs={{2,0},{3,1},{4,2},{5,3},{6,4},{7,5},{8,6},{9,7},{10,8},{11,9},{12,... | collective-permute-start | bytes 786440 | tf_op jit(solution)/shard_map/while/body/eval_jaxpr/ppermute | solution.py:14
  411.1 16.2 %collective-permute-start.4 = (bf16[64,2048]{1,0:T(8,128)(2,1)S(1)}, bf16[64,2048]{1,0:T(8,128)(2,1)S(1)}, u32[]{:S(2)}, u32[]{:S(2)}) collective-permute-start(bf16[64,2048]{1,0:T(8,128)(2,1)S(1)} %get-tuple-element.651), channel_id=1, source_target_pairs={{1,0},{2,1},{3,2},{4,3},{5,4},{6,5},{7,6},{8,7},{9,8},{10,9},{11,1... | collective-permute-start | bytes 786440 | tf_op jit(solution)/shard_map/while/body/eval_jaxpr/ppermute | solution.py:14
  441.5 12.2 %collective-permute-start = (bf16[64,2048]{1,0:T(8,128)(2,1)S(1)}, bf16[64,2048]{1,0:T(8,128)(2,1)S(1)}, u32[]{:S(2)}, u32[]{:S(2)}) collective-permute-start(bf16[64,2048]{1,0:T(8,128)(2,1)S(1)} %get-tuple-element.646), channel_id=1, source_target_pairs={{16,0},{17,1},{18,2},{19,3},{20,4},{21,5},{22,6},{23,7},{24,8},{25... | collective-permute-start | bytes 786440 | tf_op jit(solution)/shard_map/while/body/eval_jaxpr/ppermute | solution.py:14
  442.9 16.3 %collective-permute-start.1 = (bf16[64,2048]{1,0:T(8,128)(2,1)S(1)}, bf16[64,2048]{1,0:T(8,128)(2,1)S(1)}, u32[]{:S(2)}, u32[]{:S(2)}) collective-permute-start(bf16[64,2048]{1,0:T(8,128)(2,1)S(1)} %get-tuple-element.647), channel_id=1, source_target_pairs={{8,0},{9,1},{10,2},{11,3},{12,4},{13,5},{14,6},{15,7},{16,8},{17,9... | collective-permute-start | bytes 786440 | tf_op jit(solution)/shard_map/while/body/eval_jaxpr/ppermute | solution.py:14
  444.8 14.4 %collective-permute-start.2 = (bf16[64,2048]{1,0:T(8,128)(2,1)S(1)}, bf16[64,2048]{1,0:T(8,128)(2,1)S(1)}, u32[]{:S(2)}, u32[]{:S(2)}) collective-permute-start(bf16[64,2048]{1,0:T(8,128)(2,1)S(1)} %get-tuple-element.648), channel_id=1, source_target_pairs={{4,0},{5,1},{6,2},{7,3},{8,4},{9,5},{10,6},{11,7},{12,8},{13,9},{1... | collective-permute-start | bytes 786440 | tf_op jit(solution)/shard_map/while/body/eval_jaxpr/ppermute | solution.py:14
  446.8 15.4 %collective-permute-start.3 = (bf16[64,2048]{1,0:T(8,128)(2,1)S(1)}, bf16[64,2048]{1,0:T(8,128)(2,1)S(1)}, u32[]{:S(2)}, u32[]{:S(2)}) collective-permute-start(bf16[64,2048]{1,0:T(8,128)(2,1)S(1)} %get-tuple-element.649), channel_id=1, source_target_pairs={{2,0},{3,1},{4,2},{5,3},{6,4},{7,5},{8,6},{9,7},{10,8},{11,9},{12,... | collective-permute-start | bytes 786440 | tf_op jit(solution)/shard_map/while/body/eval_jaxpr/ppermute | solution.py:14
  448.7 16.2 %collective-permute-start.4 = (bf16[64,2048]{1,0:T(8,128)(2,1)S(1)}, bf16[64,2048]{1,0:T(8,128)(2,1)S(1)}, u32[]{:S(2)}, u32[]{:S(2)}) collective-permute-start(bf16[64,2048]{1,0:T(8,128)(2,1)S(1)} %get-tuple-element.651), channel_id=1, source_target_pairs={{1,0},{2,1},{3,2},{4,3},{5,4},{6,5},{7,6},{8,7},{9,8},{10,9},{11,1... | collective-permute-start | bytes 786440 | tf_op jit(solution)/shard_map/while/body/eval_jaxpr/ppermute | solution.py:14
  480.0 12.4 %collective-permute-start = (bf16[64,2048]{1,0:T(8,128)(2,1)S(1)}, bf16[64,2048]{1,0:T(8,128)(2,1)S(1)}, u32[]{:S(2)}, u32[]{:S(2)}) collective-permute-start(bf16[64,2048]{1,0:T(8,128)(2,1)S(1)} %get-tuple-element.646), channel_id=1, source_target_pairs={{16,0},{17,1},{18,2},{19,3},{20,4},{21,5},{22,6},{23,7},{24,8},{25... | collective-permute-start | bytes 786440 | tf_op jit(solution)/shard_map/while/body/eval_jaxpr/ppermute | solution.py:14
  481.4 16.7 %collective-permute-start.1 = (bf16[64,2048]{1,0:T(8,128)(2,1)S(1)}, bf16[64,2048]{1,0:T(8,128)(2,1)S(1)}, u32[]{:S(2)}, u32[]{:S(2)}) collective-permute-start(bf16[64,2048]{1,0:T(8,128)(2,1)S(1)} %get-tuple-element.647), channel_id=1, source_target_pairs={{8,0},{9,1},{10,2},{11,3},{12,4},{13,5},{14,6},{15,7},{16,8},{17,9... | collective-permute-start | bytes 786440 | tf_op jit(solution)/shard_map/while/body/eval_jaxpr/ppermute | solution.py:14
  483.4 14.8 %collective-permute-start.2 = (bf16[64,2048]{1,0:T(8,128)(2,1)S(1)}, bf16[64,2048]{1,0:T(8,128)(2,1)S(1)}, u32[]{:S(2)}, u32[]{:S(2)}) collective-permute-start(bf16[64,2048]{1,0:T(8,128)(2,1)S(1)} %get-tuple-element.648), channel_id=1, source_target_pairs={{4,0},{5,1},{6,2},{7,3},{8,4},{9,5},{10,6},{11,7},{12,8},{13,9},{1... | collective-permute-start | bytes 786440 | tf_op jit(solution)/shard_map/while/body/eval_jaxpr/ppermute | solution.py:14
  485.3 15.2 %collective-permute-start.3 = (bf16[64,2048]{1,0:T(8,128)(2,1)S(1)}, bf16[64,2048]{1,0:T(8,128)(2,1)S(1)}, u32[]{:S(2)}, u32[]{:S(2)}) collective-permute-start(bf16[64,2048]{1,0:T(8,128)(2,1)S(1)} %get-tuple-element.649), channel_id=1, source_target_pairs={{2,0},{3,1},{4,2},{5,3},{6,4},{7,5},{8,6},{9,7},{10,8},{11,9},{12,... | collective-permute-start | bytes 786440 | tf_op jit(solution)/shard_map/while/body/eval_jaxpr/ppermute | solution.py:14
  487.2 16.1 %collective-permute-start.4 = (bf16[64,2048]{1,0:T(8,128)(2,1)S(1)}, bf16[64,2048]{1,0:T(8,128)(2,1)S(1)}, u32[]{:S(2)}, u32[]{:S(2)}) collective-permute-start(bf16[64,2048]{1,0:T(8,128)(2,1)S(1)} %get-tuple-element.651), channel_id=1, source_target_pairs={{1,0},{2,1},{3,2},{4,3},{5,4},{6,5},{7,6},{8,7},{9,8},{10,9},{11,1... | collective-permute-start | bytes 786440 | tf_op jit(solution)/shard_map/while/body/eval_jaxpr/ppermute | solution.py:14
  518.7 13.4 %collective-permute-start = (bf16[64,2048]{1,0:T(8,128)(2,1)S(1)}, bf16[64,2048]{1,0:T(8,128)(2,1)S(1)}, u32[]{:S(2)}, u32[]{:S(2)}) collective-permute-start(bf16[64,2048]{1,0:T(8,128)(2,1)S(1)} %get-tuple-element.646), channel_id=1, source_target_pairs={{16,0},{17,1},{18,2},{19,3},{20,4},{21,5},{22,6},{23,7},{24,8},{25... | collective-permute-start | bytes 786440 | tf_op jit(solution)/shard_map/while/body/eval_jaxpr/ppermute | solution.py:14
  520.1 17.5 %collective-permute-start.1 = (bf16[64,2048]{1,0:T(8,128)(2,1)S(1)}, bf16[64,2048]{1,0:T(8,128)(2,1)S(1)}, u32[]{:S(2)}, u32[]{:S(2)}) collective-permute-start(bf16[64,2048]{1,0:T(8,128)(2,1)S(1)} %get-tuple-element.647), channel_id=1, source_target_pairs={{8,0},{9,1},{10,2},{11,3},{12,4},{13,5},{14,6},{15,7},{16,8},{17,9... | collective-permute-start | bytes 786440 | tf_op jit(solution)/shard_map/while/body/eval_jaxpr/ppermute | solution.py:14
  522.1 15.6 %collective-permute-start.2 = (bf16[64,2048]{1,0:T(8,128)(2,1)S(1)}, bf16[64,2048]{1,0:T(8,128)(2,1)S(1)}, u32[]{:S(2)}, u32[]{:S(2)}) collective-permute-start(bf16[64,2048]{1,0:T(8,128)(2,1)S(1)} %get-tuple-element.648), channel_id=1, source_target_pairs={{4,0},{5,1},{6,2},{7,3},{8,4},{9,5},{10,6},{11,7},{12,8},{13,9},{1... | collective-permute-start | bytes 786440 | tf_op jit(solution)/shard_map/while/body/eval_jaxpr/ppermute | solution.py:14
  524.0 15.3 %collective-permute-start.3 = (bf16[64,2048]{1,0:T(8,128)(2,1)S(1)}, bf16[64,2048]{1,0:T(8,128)(2,1)S(1)}, u32[]{:S(2)}, u32[]{:S(2)}) collective-permute-start(bf16[64,2048]{1,0:T(8,128)(2,1)S(1)} %get-tuple-element.649), channel_id=1, source_target_pairs={{2,0},{3,1},{4,2},{5,3},{6,4},{7,5},{8,6},{9,7},{10,8},{11,9},{12,... | collective-permute-start | bytes 786440 | tf_op jit(solution)/shard_map/while/body/eval_jaxpr/ppermute | solution.py:14
  525.9 16.2 %collective-permute-start.4 = (bf16[64,2048]{1,0:T(8,128)(2,1)S(1)}, bf16[64,2048]{1,0:T(8,128)(2,1)S(1)}, u32[]{:S(2)}, u32[]{:S(2)}) collective-permute-start(bf16[64,2048]{1,0:T(8,128)(2,1)S(1)} %get-tuple-element.651), channel_id=1, source_target_pairs={{1,0},{2,1},{3,2},{4,3},{5,4},{6,5},{7,6},{8,7},{9,8},{10,9},{11,1... | collective-permute-start | bytes 786440 | tf_op jit(solution)/shard_map/while/body/eval_jaxpr/ppermute | solution.py:14
  556.1 15.3 %collective-permute-start = (bf16[64,2048]{1,0:T(8,128)(2,1)S(1)}, bf16[64,2048]{1,0:T(8,128)(2,1)S(1)}, u32[]{:S(2)}, u32[]{:S(2)}) collective-permute-start(bf16[64,2048]{1,0:T(8,128)(2,1)S(1)} %get-tuple-element.646), channel_id=1, source_target_pairs={{16,0},{17,1},{18,2},{19,3},{20,4},{21,5},{22,6},{23,7},{24,8},{25... | collective-permute-start | bytes 786440 | tf_op jit(solution)/shard_map/while/body/eval_jaxpr/ppermute | solution.py:14
  557.5 19.4 %collective-permute-start.1 = (bf16[64,2048]{1,0:T(8,128)(2,1)S(1)}, bf16[64,2048]{1,0:T(8,128)(2,1)S(1)}, u32[]{:S(2)}, u32[]{:S(2)}) collective-permute-start(bf16[64,2048]{1,0:T(8,128)(2,1)S(1)} %get-tuple-element.647), channel_id=1, source_target_pairs={{8,0},{9,1},{10,2},{11,3},{12,4},{13,5},{14,6},{15,7},{16,8},{17,9... | collective-permute-start | bytes 786440 | tf_op jit(solution)/shard_map/while/body/eval_jaxpr/ppermute | solution.py:14
  559.5 17.5 %collective-permute-start.2 = (bf16[64,2048]{1,0:T(8,128)(2,1)S(1)}, bf16[64,2048]{1,0:T(8,128)(2,1)S(1)}, u32[]{:S(2)}, u32[]{:S(2)}) collective-permute-start(bf16[64,2048]{1,0:T(8,128)(2,1)S(1)} %get-tuple-element.648), channel_id=1, source_target_pairs={{4,0},{5,1},{6,2},{7,3},{8,4},{9,5},{10,6},{11,7},{12,8},{13,9},{1... | collective-permute-start | bytes 786440 | tf_op jit(solution)/shard_map/while/body/eval_jaxpr/ppermute | solution.py:14
  561.4 15.5 %collective-permute-start.3 = (bf16[64,2048]{1,0:T(8,128)(2,1)S(1)}, bf16[64,2048]{1,0:T(8,128)(2,1)S(1)}, u32[]{:S(2)}, u32[]{:S(2)}) collective-permute-start(bf16[64,2048]{1,0:T(8,128)(2,1)S(1)} %get-tuple-element.649), channel_id=1, source_target_pairs={{2,0},{3,1},{4,2},{5,3},{6,4},{7,5},{8,6},{9,7},{10,8},{11,9},{12,... | collective-permute-start | bytes 786440 | tf_op jit(solution)/shard_map/while/body/eval_jaxpr/ppermute | solution.py:14
  563.9 15.0 %collective-permute-start.4 = (bf16[64,2048]{1,0:T(8,128)(2,1)S(1)}, bf16[64,2048]{1,0:T(8,128)(2,1)S(1)}, u32[]{:S(2)}, u32[]{:S(2)}) collective-permute-start(bf16[64,2048]{1,0:T(8,128)(2,1)S(1)} %get-tuple-element.651), channel_id=1, source_target_pairs={{1,0},{2,1},{3,2},{4,3},{5,4},{6,5},{7,6},{8,7},{9,8},{10,9},{11,1... | collective-permute-start | bytes 786440 | tf_op jit(solution)/shard_map/while/body/eval_jaxpr/ppermute | solution.py:14
  580.9 194.5 %collective-permute-start.5 = (bf16[64,1024]{1,0:T(8,128)(2,1)}, bf16[64,1024]{1,0:T(8,128)(2,1)}, u32[]{:S(2)}, u32[]{:S(2)}) collective-permute-start(bf16[64,1024]{1,0:T(8,128)(2,1)} %get-tuple-element.653), channel_id=1, source_target_pairs={{32,0},{64,32},{96,64},{128,96},{160,128},{192,160},{224,192},{33,... | collective-permute-start | bytes 393224 | tf_op jit(solution)/shard_map/while/body/eval_jaxpr/ppermute | solution.py:14
  800.2 16.0 %collective-permute-start = (bf16[64,2048]{1,0:T(8,128)(2,1)S(1)}, bf16[64,2048]{1,0:T(8,128)(2,1)S(1)}, u32[]{:S(2)}, u32[]{:S(2)}) collective-permute-start(bf16[64,2048]{1,0:T(8,128)(2,1)S(1)} %get-tuple-element.646), channel_id=1, source_target_pairs={{16,0},{17,1},{18,2},{19,3},{20,4},{21,5},{22,6},{23,7},{24,8},{25... | collective-permute-start | bytes 786440 | tf_op jit(solution)/shard_map/while/body/eval_jaxpr/ppermute | solution.py:14
  801.7 19.9 %collective-permute-start.1 = (bf16[64,2048]{1,0:T(8,128)(2,1)S(1)}, bf16[64,2048]{1,0:T(8,128)(2,1)S(1)}, u32[]{:S(2)}, u32[]{:S(2)}) collective-permute-start(bf16[64,2048]{1,0:T(8,128)(2,1)S(1)} %get-tuple-element.647), channel_id=1, source_target_pairs={{8,0},{9,1},{10,2},{11,3},{12,4},{13,5},{14,6},{15,7},{16,8},{17,9... | collective-permute-start | bytes 786440 | tf_op jit(solution)/shard_map/while/body/eval_jaxpr/ppermute | solution.py:14
  803.6 18.0 %collective-permute-start.2 = (bf16[64,2048]{1,0:T(8,128)(2,1)S(1)}, bf16[64,2048]{1,0:T(8,128)(2,1)S(1)}, u32[]{:S(2)}, u32[]{:S(2)}) collective-permute-start(bf16[64,2048]{1,0:T(8,128)(2,1)S(1)} %get-tuple-element.648), channel_id=1, source_target_pairs={{4,0},{5,1},{6,2},{7,3},{8,4},{9,5},{10,6},{11,7},{12,8},{13,9},{1... | collective-permute-start | bytes 786440 | tf_op jit(solution)/shard_map/while/body/eval_jaxpr/ppermute | solution.py:14
  805.5 16.0 %collective-permute-start.3 = (bf16[64,2048]{1,0:T(8,128)(2,1)S(1)}, bf16[64,2048]{1,0:T(8,128)(2,1)S(1)}, u32[]{:S(2)}, u32[]{:S(2)}) collective-permute-start(bf16[64,2048]{1,0:T(8,128)(2,1)S(1)} %get-tuple-element.649), channel_id=1, source_target_pairs={{2,0},{3,1},{4,2},{5,3},{6,4},{7,5},{8,6},{9,7},{10,8},{11,9},{12,... | collective-permute-start | bytes 786440 | tf_op jit(solution)/shard_map/while/body/eval_jaxpr/ppermute | solution.py:14
  808.6 14.9 %collective-permute-start.4 = (bf16[64,2048]{1,0:T(8,128)(2,1)S(1)}, bf16[64,2048]{1,0:T(8,128)(2,1)S(1)}, u32[]{:S(2)}, u32[]{:S(2)}) collective-permute-start(bf16[64,2048]{1,0:T(8,128)(2,1)S(1)} %get-tuple-element.651), channel_id=1, source_target_pairs={{1,0},{2,1},{3,2},{4,3},{5,4},{6,5},{7,6},{8,7},{9,8},{10,9},{11,1... | collective-permute-start | bytes 786440 | tf_op jit(solution)/shard_map/while/body/eval_jaxpr/ppermute | solution.py:14
  863.7 18.4 %collective-permute-start = (bf16[64,2048]{1,0:T(8,128)(2,1)S(1)}, bf16[64,2048]{1,0:T(8,128)(2,1)S(1)}, u32[]{:S(2)}, u32[]{:S(2)}) collective-permute-start(bf16[64,2048]{1,0:T(8,128)(2,1)S(1)} %get-tuple-element.646), channel_id=1, source_target_pairs={{16,0},{17,1},{18,2},{19,3},{20,4},{21,5},{22,6},{23,7},{24,8},{25... | collective-permute-start | bytes 786440 | tf_op jit(solution)/shard_map/while/body/eval_jaxpr/ppermute | solution.py:14
  865.1 22.7 %collective-permute-start.1 = (bf16[64,2048]{1,0:T(8,128)(2,1)S(1)}, bf16[64,2048]{1,0:T(8,128)(2,1)S(1)}, u32[]{:S(2)}, u32[]{:S(2)}) collective-permute-start(bf16[64,2048]{1,0:T(8,128)(2,1)S(1)} %get-tuple-element.647), channel_id=1, source_target_pairs={{8,0},{9,1},{10,2},{11,3},{12,4},{13,5},{14,6},{15,7},{16,8},{17,9... | collective-permute-start | bytes 786440 | tf_op jit(solution)/shard_map/while/body/eval_jaxpr/ppermute | solution.py:14
  867.0 20.8 %collective-permute-start.2 = (bf16[64,2048]{1,0:T(8,128)(2,1)S(1)}, bf16[64,2048]{1,0:T(8,128)(2,1)S(1)}, u32[]{:S(2)}, u32[]{:S(2)}) collective-permute-start(bf16[64,2048]{1,0:T(8,128)(2,1)S(1)} %get-tuple-element.648), channel_id=1, source_target_pairs={{4,0},{5,1},{6,2},{7,3},{8,4},{9,5},{10,6},{11,7},{12,8},{13,9},{1... | collective-permute-start | bytes 786440 | tf_op jit(solution)/shard_map/while/body/eval_jaxpr/ppermute | solution.py:14
  869.0 18.9 %collective-permute-start.3 = (bf16[64,2048]{1,0:T(8,128)(2,1)S(1)}, bf16[64,2048]{1,0:T(8,128)(2,1)S(1)}, u32[]{:S(2)}, u32[]{:S(2)}) collective-permute-start(bf16[64,2048]{1,0:T(8,128)(2,1)S(1)} %get-tuple-element.649), channel_id=1, source_target_pairs={{2,0},{3,1},{4,2},{5,3},{6,4},{7,5},{8,6},{9,7},{10,8},{11,9},{12,... | collective-permute-start | bytes 786440 | tf_op jit(solution)/shard_map/while/body/eval_jaxpr/ppermute | solution.py:14
  872.1 15.7 %collective-permute-start.4 = (bf16[64,2048]{1,0:T(8,128)(2,1)S(1)}, bf16[64,2048]{1,0:T(8,128)(2,1)S(1)}, u32[]{:S(2)}, u32[]{:S(2)}) collective-permute-start(bf16[64,2048]{1,0:T(8,128)(2,1)S(1)} %get-tuple-element.651), channel_id=1, source_target_pairs={{1,0},{2,1},{3,2},{4,3},{5,4},{6,5},{7,6},{8,7},{9,8},{10,9},{11,1... | collective-permute-start | bytes 786440 | tf_op jit(solution)/shard_map/while/body/eval_jaxpr/ppermute | solution.py:14
  (98 other events, 1475.7 us)
Sparse Core Ops, SparseCore 0:
  917.9 108.3 reduce-scatter.1
